TPU v7x, 32 devices: a whole 2x2x4 slice. The times are simulated.
32 devices in a mesh: groups: 2 (over y), tile: 4 (over z), det: 2 (over x), band: 2 (over core).
Axes of the slice: x: 2, y: 2, z: 4, core: 2. Of those that a mesh axis runs over, the one named last changes fastest.
Arguments:
- left_raw: float32 [128, 512], P(('groups', 'tile'), 'det'), parts along dimension 0
- right_raw: float32 [128, 512], P(('groups', 'tile'), 'det'), parts along dimension 0
- line_offset: int32 [1024], P(('groups', 'det')), parts along dimension 0, may hold values from -8 to 8, as said below
- pair_count: int32 [8], P(('groups', 'tile')), parts along dimension 0, may hold values from 1 to 2, as said below
- pair_tile: int32 [8, 2], P(('groups', 'tile')), parts along dimension 0, may hold values from 0 to 3, as said below
- pair_base: int32 [8, 2], P(('groups', 'tile')), parts along dimension 0, may hold values from 0 to 32, as said below
Outputs:
- disparity: float32 [8, 2, 16, 512], P(('groups', 'tile'), None, 'det'), parts along dimension 0
There are 2 independent parts, one for each index of `groups`. A program takes and returns all parts, laid end to end along the dimension named above; each array names one. Nothing has to cross between parts.
Inputs may be any that keep to these rules, and one draw needn't show every extreme that they name: `line_offset`: some column has offset 8 and some column -8. `pair_count`: number of live slots of a tile; slots from this number on are empty. Some tile has 2 live slots and some tile one. `pair_tile`: every entry lies within 2 tiles of its own tile; a live slot reaches 2 tiles back, and some slot reaches 2 tiles ahead. `pair_base`: some pair has offset 32.
All inputs are finite; a program needn't handle non-finite values.
Results may differ from a plain program's by a relative error of at most 0.0003.
Values sent between devices are 32-bit elements; how exact they have to be, the bound alone decides.
No kernel may reach another device: no remote copies, remote signals or barrier semaphores. Data moves between devices by JAX's collectives and lax.ppermute only.
A program may use at most 64 MiB of HBM per device.

v0:
```python
import functools

import jax
import jax.numpy as jnp
from jax import lax
from jax.experimental import pallas as pl
from jax.experimental.pallas import tpu as pltpu
from jax.sharding import PartitionSpec as P

DISP = 128
WIN = 15
PMAX = 2
REACH = 2
OMAX = 8

REG = 0.1
SHARP = 30.0

LANES = 128
SUB = 8
BLKS = 4
STEPS = DISP // SUB
VIEWS = BLKS + STEPS - 1
GROUP = 4


def lane_gather(source, index):
    return jnp.take_along_axis(source, index, axis=1)


def row_gather(source, index):
    return jnp.take_along_axis(source, index, axis=0)


def stereo_kernel(plan, *refs):
    n_in = plan["n_in"]
    ins = refs[:n_in]
    table_any, out_ref = refs[n_in : n_in + 2]
    strip, tiles, left_rows, left_stats, raw_rows, raw_stats, right_rows, right_stats = refs[
        n_in + 2 : n_in + 10
    ]
    sums, outs, table_ref, sem = refs[n_in + 10 :]
    lines = plan["lines"]
    two_sided = plan["two_sided"]
    pad = plan["pad"]
    blocks = plan["blocks"]
    det = lax.axis_index("det")
    tile = lax.axis_index("tile")
    n_win = WIN - 1 + SUB if two_sided else SUB + WIN // 2

    copy = pltpu.make_async_copy(table_any, table_ref, sem)
    copy.start()

    lane = lax.broadcasted_iota(jnp.int32, (SUB, LANES), 1)
    row = lax.broadcasted_iota(jnp.int32, (SUB, LANES), 0)
    zero = jnp.zeros((SUB, LANES), jnp.float32)
    chunks = out_ref.shape[-1] // LANES
    per = LANES // BLKS
    for plane in range(2):
        for chunk in range(chunks):
            cols = slice(chunk * LANES, (chunk + 1) * LANES)
            strip[plane, 0:OMAX, cols] = zero
            strip[plane, OMAX + blocks * lines : 2 * OMAX + blocks * lines, cols] = zero
    if pad:
        for plane in range(2):
            for blk in range(BLKS):
                tiles[plane, blk, 0:SUB, :] = zero
                tiles[plane, blk, SUB + lines : 2 * SUB + lines, :] = zero
    offsets = plan["offsets"](ins, det)
    plan["fill"](ins, strip, tile, det)

    def resample(plane, block):
        for group in range(lines // SUB):
            start = block * lines + group * SUB
            natural = []
            for chunk in range(chunks):
                cols = slice(chunk * LANES, (chunk + 1) * LANES)
                want = row + offsets[chunk] + OMAX
                index = want & (SUB - 1)
                part = want >> 3
                picked = [
                    row_gather(
                        strip[plane, pl.ds(pl.multiple_of(start + SUB * k, SUB), SUB), cols], index
                    )
                    for k in range(3)
                ]
                natural.append(
                    jnp.where(part == 0, picked[0], jnp.where(part == 1, picked[1], picked[2]))
                )
            for blk in range(BLKS):
                index = (BLKS * lane + blk) & (LANES - 1)
                value = lane_gather(natural[0], index)
                for chunk in range(1, chunks):
                    value = jnp.where(
                        lane >= chunk * per, lane_gather(natural[chunk], index), value
                    )
                tiles[plane, blk, pad + group * SUB : pad + group * SUB + SUB, :] = value

    def row_at(win):
        if not two_sided:
            return win + det * (lines - 1 - 2 * win)
        if win < SUB + WIN // 2:
            return pad + SUB * det + win
        return pad + SUB * det - 1 - (win - SUB - WIN // 2)

    def load_row(plane, blk, win):
        return jnp.broadcast_to(tiles[plane, blk, pl.ds(row_at(win), 1), :], (SUB, LANES))

    def up(value, count):
        return jnp.where(lane >= count, pltpu.roll(value, count, 1), 0.0)

    def down(value, count):
        return jnp.where(lane < LANES - count, pltpu.roll(value, LANES - count, 1), 0.0)

    def down_wrapped(value, count):
        return jnp.where(lane >= LANES - count, pltpu.roll(value, LANES - count, 1), 0.0)

    def partials(values):
        first2 = values[0] + values[1]
        first3 = first2 + values[2]
        last2 = values[2] + values[3]
        return first2, first3, first3 + values[3], last2, values[1] + last2

    def across(values):
        first2, first3, full, last2, last3 = partials(values)
        mid = full + up(full, 1) + down(full, 1)
        return [
            mid + up(last3, 2),
            (mid + up(last2, 2)) + down(values[0], 2),
            (mid + up(values[3], 2)) + down(first2, 2),
            mid + down(first3, 2),
        ]

    def across_before(values):
        first2, first3, full, _, _ = partials(values)
        mid = down_wrapped(full, 1)
        return [
            mid,
            mid + down_wrapped(values[0], 2),
            mid + down_wrapped(first2, 2),
            mid + down_wrapped(first3, 2),
        ]

    def each_line(product):
        current = []
        for blk in range(BLKS):
            total = product(0, blk)
            for win in range(1, SUB):
                total = total + product(win, blk)
            current.append(total)
        before = None
        if two_sided:
            before = [[zero] * BLKS]
            for j in range(WIN // 2):
                before.append(
                    [
                        before[-1][blk] + product(SUB + WIN // 2 + j, blk)
                        for blk in range(BLKS)
                    ]
                )
        for line in range(SUB):
            if line:
                current = [current[blk] + product(SUB + line - 1, blk) for blk in range(BLKS)]
            if two_sided:
                yield line, [current[blk] + before[SUB - 1 - line][blk] for blk in range(BLKS)]
            else:
                yield line, current

    cell = 1.0 / (WIN * WIN)

    def stats(total, squares):
        mean = total * cell
        return mean, lax.rsqrt((squares * cell - mean * mean) + REG)

    resample(0, plan["block_of"](tile, tile))
    for win in range(n_win):
        for blk in range(BLKS):
            left_rows[win, blk] = load_row(0, blk, win)
    plain = each_line(lambda win, blk: left_rows[win, blk])
    square = each_line(lambda win, blk: left_rows[win, blk] * left_rows[win, blk])
    for (line, total), (_, squares) in zip(plain, square):
        total = across(total)
        squares = across(squares)
        for blk in range(BLKS):
            mean, gain = stats(total[blk], squares[blk])
            left_stats[0, line, blk] = mean
            left_stats[1, line, blk] = gain * SHARP
    for win in range(n_win):
        for blk in range(BLKS):
            left_rows[win, blk] = left_rows[win, blk] * cell

    copy.wait()
    for slot in range(PMAX):
        for chunk in range(chunks):
            out_ref[0, slot, :, chunk * LANES : (chunk + 1) * LANES] = zero

    def run_slot(slot, carry):
        base = table_ref[0, PMAX + slot]
        resample(1, plan["block_of"](table_ref[0, slot], tile))
        right = [[load_row(1, blk, win) for blk in range(BLKS)] for win in range(n_win)]
        for win in range(n_win):
            for blk in range(BLKS):
                raw_rows[win, blk] = right[win][blk]
        plain = each_line(lambda win, blk: right[win][blk])
        square = each_line(lambda win, blk: right[win][blk] * right[win][blk])
        for (line, total), (_, squares) in zip(plain, square):
            for part, function in enumerate((across, across_before)):
                part_total = function(total)
                part_squares = function(squares)
                for blk in range(BLKS):
                    mean, gain = stats(part_total[blk], part_squares[blk])
                    raw_stats[part, 0, line, blk] = mean
                    raw_stats[part, 1, line, blk] = gain

        def make_view(view, carry):
            shift = view - (STEPS - 1) - base
            blk = shift & (BLKS - 1)
            moved = (blk - shift) >> 2
            turn = moved + (STEPS // BLKS) * row
            wraps = lane >= LANES - turn
            source = (lane - turn) & (LANES - 1)

            def turned(value):
                return lane_gather(value, source)

            for win in range(n_win):
                right_rows[view, win] = turned(jnp.where(wraps, 0.0, raw_rows[win, blk]))
            for kind in range(2):
                for line in range(SUB):
                    right_stats[view, kind, line] = turned(
                        jnp.where(
                            wraps, raw_stats[1, kind, line, blk], raw_stats[0, kind, line, blk]
                        )
                    )
            return carry

        lax.fori_loop(0, VIEWS, make_view, 0, unroll=True)
        for line in range(SUB):
            for blk in range(BLKS):
                sums[0, line, blk] = zero
                sums[1, line, blk] = zero

        def step_body(group, carry):
            first = group * GROUP
            views = range(BLKS + GROUP - 1)

            def add(totals, win):
                left = [left_rows[win, blk] for blk in range(BLKS)]
                right = [right_rows[first + view, win] for view in views]
                terms = [
                    [left[blk] * right[step + blk] for blk in range(BLKS)] for step in range(GROUP)
                ]
                if totals is None:
                    return terms
                return [[t + v for t, v in zip(*pair)] for pair in zip(totals, terms)]

            current = None
            for win in range(SUB):
                current = add(current, win)
            before = [None]
            if two_sided:
                for j in range(WIN // 2):
                    before.append(add(before[-1], SUB + WIN // 2 + j))
            for line in range(SUB):
                if line:
                    current = add(current, SUB + line - 1)
                values = current
                if two_sided and line < SUB - 1:
                    values = [
                        [t + v for t, v in zip(*pair)]
                        for pair in zip(current, before[SUB - 1 - line])
                    ]
                mean_l = [left_stats[0, line, blk] for blk in range(BLKS)]
                gain_l = [left_stats[1, line, blk] for blk in range(BLKS)]
                mean_r = [right_stats[first + view, 0, line] for view in views]
                gain_r = [right_stats[first + view, 1, line] for view in views]
                weights = [sums[0, line, blk] for blk in range(BLKS)]
                moments = [sums[1, line, blk] for blk in range(BLKS)]
                for step in range(GROUP):
                    for blk, total in enumerate(across(values[step])):
                        cov = total - mean_l[blk] * mean_r[step + blk]
                        weight = jnp.exp((cov * gain_l[blk]) * gain_r[step + blk])
                        moments[blk] = moments[blk] + weights[blk]
                        weights[blk] = weights[blk] + weight
                for blk in range(BLKS):
                    sums[0, line, blk] = weights[blk]
                    sums[1, line, blk] = moments[blk]
            return carry

        lax.fori_loop(0, STEPS // GROUP, step_body, 0, unroll=True)
        scale = (row * STEPS).astype(jnp.float32)
        for line in range(SUB):
            for blk in range(BLKS):
                weights = sums[0, line, blk]
                moments = sums[1, line, blk] + scale * weights
                weight_sum = jnp.sum(weights, axis=0, keepdims=True)
                moment_sum = jnp.sum(moments, axis=0, keepdims=True)
                value = (base.astype(jnp.float32) + moment_sum / weight_sum) / DISP
                target = line if two_sided else line + det * (SUB - 1 - 2 * line)
                outs[blk, pl.ds(target, 1), :] = value
        for chunk in range(chunks):
            index = chunk * per + (lane >> 2)
            value = lane_gather(outs[0], index)
            for blk in range(1, BLKS):
                value = jnp.where(
                    (lane & (BLKS - 1)) == blk, lane_gather(outs[blk], index), value
                )
            out_ref[0, slot, :, chunk * LANES : (chunk + 1) * LANES] = value
        return carry

    lax.fori_loop(0, jnp.minimum(table_ref[0, 2 * PMAX], PMAX), run_slot, 0)


def run_kernel(plan, ins, pair_count, pair_tile, pair_base, cols):
    lines = plan["lines"]
    blocks = plan["blocks"]
    n_win = WIN - 1 + SUB if plan["two_sided"] else SUB + WIN // 2
    plan = dict(plan, n_in=len(ins))
    vmem = pl.BlockSpec(memory_space=pltpu.VMEM)
    anywhere = pl.BlockSpec(memory_space=pl.ANY)
    table = jnp.concatenate([pair_tile, pair_base, pair_count[None]], axis=1)
    f32 = jnp.float32
    return pl.pallas_call(
        functools.partial(stereo_kernel, plan),
        out_shape=jax.ShapeDtypeStruct((1, PMAX, SUB, cols), f32),
        in_specs=[vmem] * len(ins) + [anywhere],
        out_specs=vmem,
        scratch_shapes=[
            pltpu.VMEM((2, blocks * lines + 2 * OMAX, cols), f32),
            pltpu.VMEM((2, BLKS, lines + 2 * plan["pad"], LANES), f32),
            pltpu.VMEM((n_win, BLKS, SUB, LANES), f32),
            pltpu.VMEM((2, SUB, BLKS, SUB, LANES), f32),
            pltpu.VMEM((n_win, BLKS, SUB, LANES), f32),
            pltpu.VMEM((2, 2, SUB, BLKS, SUB, LANES), f32),
            pltpu.VMEM((VIEWS, n_win, SUB, LANES), f32),
            pltpu.VMEM((VIEWS, 2, SUB, SUB, LANES), f32),
            pltpu.VMEM((2, SUB, BLKS, SUB, LANES), f32),
            pltpu.VMEM((BLKS, SUB, LANES), f32),
            pltpu.SMEM(table.shape, jnp.int32),
            pltpu.SemaphoreType.DMA,
        ],
        compiler_params=pltpu.CompilerParams(vmem_limit_bytes=32 << 20),
        name="stereo",
    )(*ins, table)


def xor_front(left_raw, right_raw, line_offset):
    tiles, dets, bands = (lax.axis_size(a) for a in ("tile", "det", "band"))
    lines, width = left_raw.shape

    def fetch(value, flip):
        pairs = []
        for t in range(tiles):
            for d in range(dets):
                for b in range(bands):
                    source = (t * dets + d) * bands + b
                    target = ((t ^ flip) * dets + (d ^ b)) * bands + b
                    pairs.append((source, target))
        return lax.ppermute(value, ("tile", "det", "band"), pairs)

    swap = [(0, 1), (1, 0)]
    both = jnp.concatenate([left_raw, right_raw])
    far, mid, near = (fetch(both, flip) for flip in (3, 2, 1))
    held, line_offset = lax.optimization_barrier((both, line_offset))
    spread = jnp.broadcast_to(line_offset.astype(jnp.float32)[None], (SUB, width))
    slab = jnp.concatenate([held, spread])
    beside = lax.ppermute(slab, "det", swap)
    far2, mid2, near2 = (lax.ppermute(v, "band", swap) for v in (far, mid, near))
    ins = [slab, beside, mid, mid2, near, near2, far, far2]

    def fill(ins, strip, tile, det):
        band = lax.axis_index("band")

        def place(ref, plane, flip, side):
            rows = pl.ds(pl.multiple_of(OMAX + (tile ^ flip) * lines, SUB), lines)
            half = pl.ds(pl.multiple_of((det ^ side) * width, LANES), width)
            strip[plane, rows, half] = ref[plane * lines : (plane + 1) * lines, :]

        slab, beside, mid, mid2, near, near2, far, far2 = ins
        for plane in range(2):
            place(slab, plane, 0, 0)
            place(beside, plane, 0, 1)
            for first, second, flip in ((far, far2, 3), (near, near2, 1), (mid, mid2, 2)):
                if plane or flip != 2:
                    place(first, plane, flip, band)
                    place(second, plane, flip, 1 - band)

    def offsets(ins, det):
        own, other = ins[0], ins[1]
        per = width // LANES
        result = []
        for chunk in range(dets * per):
            cols = slice((chunk % per) * LANES, (chunk % per + 1) * LANES)
            rows = slice(2 * lines, 2 * lines + SUB)
            value = jnp.where(det == chunk // per, own[rows, cols], other[rows, cols])
            result.append(value.astype(jnp.int32))
        return result

    plan = dict(
        lines=lines,
        blocks=tiles,
        two_sided=False,
        pad=0,
        fill=fill,
        offsets=offsets,
        block_of=lambda partner, tile: partner,
    )
    return plan, ins, dets * width


def shift_front(left_raw, right_raw, line_offset):
    count, dets = lax.axis_size("tile"), lax.axis_size("det")
    lines, width = left_raw.shape
    reach = REACH + 1
    own = lax.all_gather(jnp.stack([left_raw, right_raw]), "det")
    offset = lax.all_gather(line_offset, "det").reshape(1, dets * width)
    ins = [offset]
    for shift in range(-reach, reach + 1):
        if shift:
            pairs = [(i, i - shift) for i in range(count) if 0 <= i - shift < count]
            ins.append(lax.ppermute(own, "tile", pairs))
        else:
            ins.append(own)

    def fill(ins, strip, tile, det):
        for j in range(2 * reach + 1):
            rows = slice(OMAX + j * lines, OMAX + (j + 1) * lines)
            for h in range(dets):
                for plane in range(2):
                    strip[plane, rows, h * width : (h + 1) * width] = ins[1 + j][h, plane]

    def offsets(ins, det):
        return [
            jnp.broadcast_to(ins[0][0:1, c * LANES : (c + 1) * LANES], (SUB, LANES))
            for c in range(dets * width // LANES)
        ]

    plan = dict(
        lines=lines,
        blocks=2 * reach + 1,
        two_sided=True,
        pad=SUB,
        fill=fill,
        offsets=offsets,
        block_of=lambda partner, tile: partner - tile + reach,
    )
    return plan, ins, dets * width


def shards(left_raw, right_raw, line_offset, pair_count, pair_tile, pair_base):
    sizes = tuple(lax.axis_size(a) for a in ("tile", "det", "band"))
    front = xor_front if sizes == (4, 2, 2) else shift_front
    plan, ins, cols = front(left_raw, right_raw, line_offset)
    return run_kernel(plan, ins, pair_count, pair_tile, pair_base, cols)


def solution(mesh):
    return jax.shard_map(
        shards,
        mesh=mesh,
        in_specs=(
            P(("groups", "tile"), "det"),
            P(("groups", "tile"), "det"),
            P(("groups", "det")),
            P(("groups", "tile")),
            P(("groups", "tile"), None),
            P(("groups", "tile"), None),
        ),
        out_specs=P(("groups", "tile"), None, "det", None),
        check_vma=False,
    )
```

profile of v0, /device:TPU:9, one launch (start us, length us, event | category | flops | bytes accessed | tf_op | source)
XLA Modules:
  0.0 17.7 jit_solution(13519124715721910311)
XLA Ops:
  0.0 0.0 copy-start
  0.0 0.7 %constant_dynamic-update-slice_fusion.1 = f32[32,256]{1,0:T(8,128)S(1)} fusion(f32[16,256]{1,0:T(8,128)} %param.6), kind=kLoop, calls=%fused_computation.2 | loop fusion | bytes 32768
  0.7 0.0 copy-done
  0.7 2.3 %collective-permute-start.5 = (f32[32,256]{1,0:T(8,128)S(1)}, f32[32,256]{1,0:T(8,128)S(1)}, u32[]{:S(2)}, u32[]{:S(2)}) collective-permute-start(f32[32,256]{1,0:T(8,128)S(1)} %constant_dynamic-update-slice_fusion), channel_id=1, source_target_pairs={{0,12},{1,15},{2,14},{3,13},{4,8},{5,11},{6,10},{7,9},{8,4},{9,7},... | collective-permute-start | bytes 98312 | tf_op jit(solution)/shard_map/ppermute | solution.py:359
  3.0 2.2 %collective-permute-start.3 = (f32[32,256]{1,0:T(8,128)S(1)}, f32[32,256]{1,0:T(8,128)S(1)}, u32[]{:S(2)}, u32[]{:S(2)}) collective-permute-start(f32[32,256]{1,0:T(8,128)S(1)} %constant_dynamic-update-slice_fusion), channel_id=1, source_target_pairs={{0,4},{1,7},{2,6},{3,5},{4,0},{5,3},{6,2},{7,1},{8,12},{9,15},{10,... | collective-permute-start | bytes 98312 | tf_op jit(solution)/shard_map/ppermute | solution.py:359
  5.2 0.1 collective-permute-start.1
  5.3 0.0 copy-done.1
  5.3 1.2 %collective-permute-start = (f32[40,256]{1,0:T(8,128)S(1)}, f32[40,256]{1,0:T(8,128)S(1)}, u32[]{:S(2)}, u32[]{:S(2)}) collective-permute-start(f32[40,256]{1,0:T(8,128)S(1)} %pad_maximum_fusion.refs_0_), channel_id=1, source_target_pairs={{0,2},{2,0},{1,3},{3,1},{4,6},{6,4},{5,7},{7,5},{8,10},{10,8},{9,1... | collective-permute-start | bytes 122888 | tf_op jit(solution)/shard_map/ppermute | solution.py:367
  7.2 0.0 copy-start.2
  7.2 0.0 copy-start.3
  7.2 0.0 collective-permute-done.5.refs_6_
  7.2 0.7 %collective-permute-start.6 = (f32[32,256]{1,0:T(8,128)S(1)}, f32[32,256]{1,0:T(8,128)S(1)}, u32[]{:S(2)}, u32[]{:S(2)}) collective-permute-start(f32[32,256]{1,0:T(8,128)S(1)} %collective-permute-done.5.refs_6_), channel_id=1, source_target_pairs={{0,1},{1,0},{2,3},{3,2},{4,5},{5,4},{6,7},{7,6},{8,9},{9,8},{10,11... | collective-permute-start | bytes 98312 | tf_op jit(solution)/shard_map/ppermute | solution.py:368
  7.9 0.0 collective-permute-done.3.refs_4_
  7.9 0.6 %collective-permute-start.4 = (f32[32,256]{1,0:T(8,128)S(1)}, f32[32,256]{1,0:T(8,128)S(1)}, u32[]{:S(2)}, u32[]{:S(2)}) collective-permute-start(f32[32,256]{1,0:T(8,128)S(1)} %collective-permute-done.3.refs_4_), channel_id=1, source_target_pairs={{0,1},{1,0},{2,3},{3,2},{4,5},{5,4},{6,7},{7,6},{8,9},{9,8},{10,11... | collective-permute-start | bytes 98312 | tf_op jit(solution)/shard_map/ppermute | solution.py:368
  8.5 1.3 %collective-permute-done.1.refs_2_ = f32[32,256]{1,0:T(8,128)S(1)} collective-permute-done((f32[32,256]{1,0:T(8,128)S(1)}, f32[32,256]{1,0:T(8,128)S(1)}, u32[]{:S(2)}, u32[]{:S(2)}) %collective-permute-start.1) | collective-permute-done | bytes 32800 | tf_op jit(solution)/shard_map/ppermute | solution.py:359
  9.8 0.8 %collective-permute-start.2 = (f32[32,256]{1,0:T(8,128)S(1)}, f32[32,256]{1,0:T(8,128)S(1)}, u32[]{:S(2)}, u32[]{:S(2)}) collective-permute-start(f32[32,256]{1,0:T(8,128)S(1)} %collective-permute-done.1.refs_2_), channel_id=1, source_target_pairs={{0,1},{1,0},{2,3},{3,2},{4,5},{5,4},{6,7},{7,6},{8,9},{9,8},{10,11... | collective-permute-start | bytes 98312 | tf_op jit(solution)/shard_map/ppermute | solution.py:368
  10.6 0.0 copy-done.2
  10.6 0.0 copy-done.3
  10.6 0.1 pad_add_fusion.refs_8_
  10.7 0.0 collective-permute-done.refs_1_
  10.7 0.0 collective-permute-done.6.refs_7_
  10.7 0.0 collective-permute-done.4.refs_5_
  10.7 0.8 %collective-permute-done.2.refs_3_ = f32[32,256]{1,0:T(8,128)S(1)} collective-permute-done((f32[32,256]{1,0:T(8,128)S(1)}, f32[32,256]{1,0:T(8,128)S(1)}, u32[]{:S(2)}, u32[]{:S(2)}) %collective-permute-start.2) | collective-permute-done | bytes 32800 | tf_op jit(solution)/shard_map/ppermute | solution.py:368
  11.4 6.3 %stereo.1 = f32[1,2,8,512]{3,2,1,0:T(8,128)} custom-call(f32[40,256]{1,0:T(8,128)S(1)} %pad_maximum_fusion.refs_0_, f32[40,256]{1,0:T(8,128)S(1)} %collective-permute-done.refs_1_, f32[32,256]{1,0:T(8,128)S(1)} %collective-permute-done.1.refs_2_, f32[32,256]{1,0:T(8,128)S(1)} %collective-permute-done.2.refs_3_, ...), custom_call_target="tpu_custom_call" | custom-call | tf_op jit(solution)/shard_map/stereo/pallas_call | solution.py:323
  (5 shorter events, 0.0 us)
Async XLA Ops:
  0.0 0.7 %copy-start = (f32[16,256]{1,0:T(8,128)S(1)}, f32[16,256]{1,0:T(8,128)}, u32[]{:S(2)}) copy-start(f32[16,256]{1,0:T(8,128)} %param.7) | copy-start | bytes 49156
  0.7 4.5 %copy-start.1 = (s32[256]{0:T(256)S(1)}, s32[256]{0:T(256)}, u32[]{:S(2)}) copy-start(s32[256]{0:T(256)} %param.8) | copy-start | bytes 3076
  0.7 6.4 %collective-permute-start.5 = (f32[32,256]{1,0:T(8,128)S(1)}, f32[32,256]{1,0:T(8,128)S(1)}, u32[]{:S(2)}, u32[]{:S(2)}) collective-permute-start(f32[32,256]{1,0:T(8,128)S(1)} %constant_dynamic-update-slice_fusion), channel_id=1, source_target_pairs={{0,12},{1,15},{2,14},{3,13},{4,8},{5,11},{6,10},{7,9},{8,4},{9,7},... | collective-permute-start | bytes 98312 | tf_op jit(solution)/shard_map/ppermute | solution.py:359
  3.0 4.8 %collective-permute-start.3 = (f32[32,256]{1,0:T(8,128)S(1)}, f32[32,256]{1,0:T(8,128)S(1)}, u32[]{:S(2)}, u32[]{:S(2)}) collective-permute-start(f32[32,256]{1,0:T(8,128)S(1)} %constant_dynamic-update-slice_fusion), channel_id=1, source_target_pairs={{0,4},{1,7},{2,6},{3,5},{4,0},{5,3},{6,2},{7,1},{8,12},{9,15},{10,... | collective-permute-start | bytes 98312 | tf_op jit(solution)/shard_map/ppermute | solution.py:359
  5.2 4.6 %collective-permute-start.1 = (f32[32,256]{1,0:T(8,128)S(1)}, f32[32,256]{1,0:T(8,128)S(1)}, u32[]{:S(2)}, u32[]{:S(2)}) collective-permute-start(f32[32,256]{1,0:T(8,128)S(1)} %constant_dynamic-update-slice_fusion), channel_id=1, source_target_pairs={{0,8},{1,11},{2,10},{3,9},{4,12},{5,15},{6,14},{7,13},{8,0},{9,3},... | collective-permute-start | bytes 98312 | tf_op jit(solution)/shard_map/ppermute | solution.py:359
  5.3 5.3 %collective-permute-start = (f32[40,256]{1,0:T(8,128)S(1)}, f32[40,256]{1,0:T(8,128)S(1)}, u32[]{:S(2)}, u32[]{:S(2)}) collective-permute-start(f32[40,256]{1,0:T(8,128)S(1)} %pad_maximum_fusion.refs_0_), channel_id=1, source_target_pairs={{0,2},{2,0},{1,3},{3,1},{4,6},{6,4},{5,7},{7,5},{8,10},{10,8},{9,1... | collective-permute-start | bytes 122888 | tf_op jit(solution)/shard_map/ppermute | solution.py:367
  7.2 3.4 %copy-start.2 = (s32[1,2]{1,0:T(1,128)S(1)}, s32[1,2]{1,0:T(1,128)}, u32[]{:S(2)}) copy-start(s32[1,2]{1,0:T(1,128)} %param.11) | copy-start | bytes 28
  7.2 3.4 %copy-start.3 = (s32[1,2]{1,0:T(1,128)S(1)}, s32[1,2]{1,0:T(1,128)}, u32[]{:S(2)}) copy-start(s32[1,2]{1,0:T(1,128)} %param.10) | copy-start | bytes 28
  7.2 3.5 %collective-permute-start.6 = (f32[32,256]{1,0:T(8,128)S(1)}, f32[32,256]{1,0:T(8,128)S(1)}, u32[]{:S(2)}, u32[]{:S(2)}) collective-permute-start(f32[32,256]{1,0:T(8,128)S(1)} %collective-permute-done.5.refs_6_), channel_id=1, source_target_pairs={{0,1},{1,0},{2,3},{3,2},{4,5},{5,4},{6,7},{7,6},{8,9},{9,8},{10,11... | collective-permute-start | bytes 98312 | tf_op jit(solution)/shard_map/ppermute | solution.py:368
  7.9 2.8 %collective-permute-start.4 = (f32[32,256]{1,0:T(8,128)S(1)}, f32[32,256]{1,0:T(8,128)S(1)}, u32[]{:S(2)}, u32[]{:S(2)}) collective-permute-start(f32[32,256]{1,0:T(8,128)S(1)} %collective-permute-done.3.refs_4_), channel_id=1, source_target_pairs={{0,1},{1,0},{2,3},{3,2},{4,5},{5,4},{6,7},{7,6},{8,9},{9,8},{10,11... | collective-permute-start | bytes 98312 | tf_op jit(solution)/shard_map/ppermute | solution.py:368
  9.8 1.7 %collective-permute-start.2 = (f32[32,256]{1,0:T(8,128)S(1)}, f32[32,256]{1,0:T(8,128)S(1)}, u32[]{:S(2)}, u32[]{:S(2)}) collective-permute-start(f32[32,256]{1,0:T(8,128)S(1)} %collective-permute-done.1.refs_2_), channel_id=1, source_target_pairs={{0,1},{1,0},{2,3},{3,2},{4,5},{5,4},{6,7},{7,6},{8,9},{9,8},{10,11... | collective-permute-start | bytes 98312 | tf_op jit(solution)/shard_map/ppermute | solution.py:368
where the time goes:
time: 18.1 us; the launch traced here: 17.7 us
  starting transfers between devices  7.82 us (43%)
  Pallas kernels  6.31 us (35%)
  waiting for transfers between devices  2.07 us (11%)
  local copies, waits for them, and re-layouts  0.76 us (4%)
  between operations  0.7 us (4%)
    pallas_call x1, Pallas kernels, run_kernel(): pl.pallas_call(functools.partial(stereo_kernel, plan), out_shape=jax.Shap...  6.31 us
    ppermute x3, starting transfers between devices, fetch(): return lax.ppermute(value, ('tile', 'det', 'band'), pairs)  4.54 us
    ppermute x3, starting transfers between devices, xor_front(): lax.ppermute(v, 'band', swap)  2.08 us
    ppermute x3, waiting for transfers between devices, fetch(): return lax.ppermute(value, ('tile', 'det', 'band'), pairs)  1.29 us
    ppermute x1, starting transfers between devices, xor_front(): beside = lax.ppermute(slab, 'det', swap)  1.21 us
    ppermute x3, waiting for transfers between devices, xor_front(): lax.ppermute(v, 'band', swap)  0.77 us
    unnamed x9, local copies, waits for them, and re-layouts  0.75 us
  transfers between devices with their start and end apart: 7, of which 2 were waited for; matrix products, arithmetic and copies ran while one was open for 1% of the time, Pallas kernels for 0%

commit v1 on v0

v1 whole, which is shorter than its diff:
```python
import functools

import jax
import jax.numpy as jnp
from jax import lax
from jax.experimental import pallas as pl
from jax.experimental.pallas import tpu as pltpu
from jax.sharding import PartitionSpec as P

DISP = 128
WIN = 15
PMAX = 2
REACH = 2
OMAX = 8

REG = 0.1
SHARP = 30.0

LANES = 128
SUB = 8
BLKS = 8
SPOTS = LANES // 2
STEPS = 8
SIDE = WIN // 2
VIEWS = BLKS + STEPS - 1
TOGETHER = 4


def lane_gather(source, index):
    return jnp.take_along_axis(source, index, axis=1)


def row_gather(source, index):
    return jnp.take_along_axis(source, index, axis=0)


def stereo_kernel(plan, *refs):
    n_in = plan["n_in"]
    ins = refs[:n_in]
    table_any, out_ref = refs[n_in : n_in + 2]
    strip, tiles, left_rows, left_stats, raw_rows, raw_stats = refs[n_in + 2 : n_in + 8]
    right_rows, right_stats, outs, table_ref, sem = refs[n_in + 8 :]
    lines = plan["lines"]
    two_sided = plan["two_sided"]
    pad = plan["pad"]
    blocks = plan["blocks"]
    det = lax.axis_index("det")
    tile = lax.axis_index("tile")
    n_win = SUB + 2 * SIDE if two_sided else SUB + SIDE

    copy = pltpu.make_async_copy(table_any, table_ref, sem)
    copy.start()

    lane = lax.broadcasted_iota(jnp.int32, (SUB, LANES), 1)
    row = lax.broadcasted_iota(jnp.int32, (SUB, LANES), 0)
    zero = jnp.zeros((SUB, LANES), jnp.float32)
    chunks = out_ref.shape[-1] // LANES
    per = LANES // BLKS
    spot = lane & (SPOTS - 1)
    half = lane >> 6
    for plane in range(2):
        for chunk in range(chunks):
            cols = slice(chunk * LANES, (chunk + 1) * LANES)
            strip[plane, 0:OMAX, cols] = zero
            strip[plane, OMAX + blocks * lines : 2 * OMAX + blocks * lines, cols] = zero
    if pad:
        for plane in range(2):
            for blk in range(BLKS):
                tiles[plane, blk, 0:SUB, :] = zero
                tiles[plane, blk, SUB + lines : 2 * SUB + lines, :] = zero
    offsets = plan["offsets"](ins, det)
    plan["fill"](ins, strip, tile, det)

    def resample(plane, block):
        for group in range(lines // SUB):
            start = block * lines + group * SUB
            natural = []
            for chunk in range(chunks):
                cols = slice(chunk * LANES, (chunk + 1) * LANES)
                want = row + offsets[chunk] + OMAX
                index = want & (SUB - 1)
                part = want >> 3
                picked = [
                    row_gather(
                        strip[plane, pl.ds(pl.multiple_of(start + SUB * k, SUB), SUB), cols], index
                    )
                    for k in range(3)
                ]
                natural.append(
                    jnp.where(part == 0, picked[0], jnp.where(part == 1, picked[1], picked[2]))
                )
            for blk in range(BLKS):
                index = (BLKS * spot + blk) & (LANES - 1)
                value = lane_gather(natural[0], index)
                for chunk in range(1, chunks):
                    value = jnp.where(
                        spot >= chunk * per, lane_gather(natural[chunk], index), value
                    )
                tiles[plane, blk, pad + group * SUB : pad + group * SUB + SUB, :] = value

    def row_at(win):
        if not two_sided:
            return win + det * (lines - 1 - 2 * win)
        if win < SUB + SIDE:
            return pad + SUB * det + win
        return pad + SUB * det - 1 - (win - SUB - SIDE)

    def load_row(ref, blk, win):
        return jnp.broadcast_to(ref[blk, pl.ds(row_at(win), 1), :], (SUB, LANES))

    def before(value):
        return pltpu.roll(value, 1, 1)

    def after(value):
        return pltpu.roll(value, LANES - 1, 1)

    def window_parts(wide):
        core = wide[SIDE]
        for blk in range(1, BLKS):
            core = core + wide[SIDE + blk]
        low, high = [None] * BLKS, [None] * BLKS
        for k in range(SIDE):
            value = wide[SIDE - 1 - k]
            low[BLKS - 2 - k] = value if k == 0 else low[BLKS - 1 - k] + value
            value = wide[SIDE + BLKS + k]
            high[k + 1] = value if k == 0 else high[k] + value
        return core, low, high

    def plus(first, second):
        return first if second is None else first + second

    def across(inner):
        first, last = [inner[0]], [inner[-1]]
        for k in range(1, BLKS):
            first.append(first[-1] + inner[k])
            if k < SIDE:
                last.append(last[-1] + inner[BLKS - 1 - k])
        result = [first[-1]] * BLKS
        for k in range(SIDE):
            low = jnp.where(spot >= 1, before(last[k]), 0.0)
            high = jnp.where(spot < SPOTS - 1, after(first[k]), 0.0)
            result[BLKS - 2 - k] = result[BLKS - 2 - k] + low
            result[k + 1] = result[k + 1] + high
        return result

    cell = 1.0 / (WIN * WIN)

    def tile_stats(rows, gain_scale):
        totals = []
        for square in (False, True):
            columns = []
            for blk in range(BLKS):
                total = None
                for win in range(n_win):
                    value = rows[win][blk]
                    if square:
                        value = value * value
                    if win >= SUB + SIDE:
                        value = jnp.where(row < SUB - 1 - (win - SUB - SIDE), value, 0.0)
                    elif win >= SUB:
                        value = jnp.where(row > win - SUB, value, 0.0)
                    total = plus(value, total)
                columns.append(total)
            wide = [
                jnp.where(spot >= 1, before(columns[blk]), 0.0) for blk in range(1, BLKS)
            ] + columns + [after(columns[blk]) for blk in range(BLKS - 1)]
            core, low, high = window_parts(wide)
            main, ahead = [], []
            for blk in range(BLKS):
                value = plus(core, low[blk])
                if high[blk] is None:
                    ahead.append(zero)
                else:
                    value = value + jnp.where(spot < SPOTS - 1, high[blk], 0.0)
                    ahead.append(jnp.where(spot == SPOTS - 1, high[blk], 0.0))
                main.append(value)
            totals.append((main, ahead))
        result = []
        for part in range(2):
            means, gains = [], []
            for blk in range(BLKS):
                mean = totals[0][part][blk] * cell
                variance = totals[1][part][blk] * cell - mean * mean
                means.append(mean)
                gains.append(lax.rsqrt(variance + REG) * gain_scale)
            result.append((means, gains))
        return result

    resample(0, plan["block_of"](tile, tile))
    left = [[load_row(tiles.at[0], blk, win) for blk in range(BLKS)] for win in range(n_win)]
    for kind, values in enumerate(tile_stats(left, SHARP)[0]):
        for blk in range(BLKS):
            for line in range(SUB):
                left_stats[kind, line, blk] = jnp.broadcast_to(
                    values[blk][line : line + 1, :], (SUB, LANES)
                )
    for win in range(n_win):
        for blk in range(BLKS):
            left_rows[win, blk] = left[win][blk] * cell

    copy.wait()
    for slot in range(PMAX):
        for chunk in range(chunks):
            out_ref[0, slot, :, chunk * LANES : (chunk + 1) * LANES] = zero

    def run_slot(slot, carry):
        base = table_ref[0, PMAX + slot]
        resample(1, plan["block_of"](table_ref[0, slot], tile))
        right = [[load_row(tiles.at[1], blk, win) for blk in range(BLKS)] for win in range(n_win)]
        for win in range(n_win):
            for blk in range(BLKS):
                raw_rows[win, blk] = right[win][blk]
        for part, pair in enumerate(tile_stats(right, 1.0)):
            for kind, values in enumerate(pair):
                for blk in range(BLKS):
                    raw_stats[part, kind, blk] = values[blk]

        for view in range(VIEWS):
            shift = view - (STEPS - 1) - base
            blk = shift & (BLKS - 1)
            turn = ((blk - shift) >> 3) + half + 2 * row
            wraps = spot >= SPOTS - turn
            source = ((lane - turn) & (SPOTS - 1)) + SPOTS * half
            for win in range(n_win):
                value = jnp.where(wraps, 0.0, raw_rows[win, blk])
                right_rows[view, win] = lane_gather(value, source)
            for kind in range(2):
                for line in range(SUB):
                    main, ahead = (
                        jnp.broadcast_to(
                            raw_stats[part, kind, blk, pl.ds(line, 1), :], (SUB, LANES)
                        )
                        for part in range(2)
                    )
                    right_stats[view, kind, line] = lane_gather(
                        jnp.where(wraps, ahead, main), source
                    )

        def add(totals, win, first, count):
            left = [left_rows[win, blk] for blk in range(BLKS)]
            right = [right_rows[first + view, win] for view in range(BLKS + count - 1)]
            terms = [[left[blk] * right[step + blk] for blk in range(BLKS)] for step in range(count)]
            return terms if totals is None else sums_of(totals, terms)

        def sums_of(totals, terms):
            return [[t + v for t, v in zip(*pair)] for pair in zip(totals, terms)]

        current = []
        for first in range(0, STEPS, TOGETHER):
            totals = None
            for win in range(SUB):
                totals = add(totals, win, first, TOGETHER)
            current += totals
        lower = [None]
        if two_sided:
            for j in range(SIDE):
                lower.append(add(lower[-1], SUB + SIDE + j, 0, STEPS))
        scale = (2 * BLKS * row + BLKS * half).astype(jnp.float32)
        for line in range(SUB):
            left = [left_rows[SUB + line - 1, blk] for blk in range(BLKS)]
            right = [right_rows[view, SUB + line - 1] for view in range(VIEWS)]
            mean_l = [left_stats[0, line, blk] for blk in range(BLKS)]
            gain_l = [left_stats[1, line, blk] for blk in range(BLKS)]
            weights, moments = [None] * BLKS, [None] * BLKS
            for step in range(STEPS):
                if line:
                    current[step] = [
                        current[step][blk] + left[blk] * right[step + blk] for blk in range(BLKS)
                    ]
                values = current[step]
                if two_sided and line < SUB - 1:
                    values = sums_of([values], [lower[SUB - 1 - line][step]])[0]
                mean_r = [right_stats[step + blk, 0, line] for blk in range(BLKS)]
                gain_r = [right_stats[step + blk, 1, line] for blk in range(BLKS)]
                for blk, total in enumerate(across(values)):
                    cov = total - mean_l[blk] * mean_r[blk]
                    weight = jnp.exp((cov * gain_l[blk]) * gain_r[blk])
                    if step == 0:
                        weights[blk] = weight
                    else:
                        moments[blk] = plus(weights[blk], moments[blk])
                        weights[blk] = weights[blk] + weight
            target = pl.ds(line if two_sided else line + det * (SUB - 1 - 2 * line), 1)
            for blk in range(BLKS):
                moment = moments[blk] + scale * weights[blk]
                outs[0, blk, target, :] = jnp.sum(weights[blk], axis=0, keepdims=True)
                outs[1, blk, target, :] = jnp.sum(moment, axis=0, keepdims=True)
        values = []
        for blk in range(BLKS):
            weights, moments = (v + pltpu.roll(v, SPOTS, 1) for v in (outs[0, blk], outs[1, blk]))
            values.append((base.astype(jnp.float32) + moments / weights) / DISP)
        for chunk in range(chunks):
            index = chunk * per + (lane >> 3)
            value = lane_gather(values[0], index)
            for blk in range(1, BLKS):
                value = jnp.where(
                    (lane & (BLKS - 1)) == blk, lane_gather(values[blk], index), value
                )
            out_ref[0, slot, :, chunk * LANES : (chunk + 1) * LANES] = value
        return carry

    lax.fori_loop(0, jnp.minimum(table_ref[0, 2 * PMAX], PMAX), run_slot, 0)


def run_kernel(plan, ins, pair_count, pair_tile, pair_base, cols):
    lines = plan["lines"]
    blocks = plan["blocks"]
    n_win = SUB + 2 * SIDE if plan["two_sided"] else SUB + SIDE
    plan = dict(plan, n_in=len(ins))
    vmem = pl.BlockSpec(memory_space=pltpu.VMEM)
    anywhere = pl.BlockSpec(memory_space=pl.ANY)
    table = jnp.concatenate([pair_tile, pair_base, pair_count[None]], axis=1)
    f32 = jnp.float32
    return pl.pallas_call(
        functools.partial(stereo_kernel, plan),
        out_shape=jax.ShapeDtypeStruct((1, PMAX, SUB, cols), f32),
        in_specs=[vmem] * len(ins) + [anywhere],
        out_specs=vmem,
        scratch_shapes=[
            pltpu.VMEM((2, blocks * lines + 2 * OMAX, cols), f32),
            pltpu.VMEM((2, BLKS, lines + 2 * plan["pad"], LANES), f32),
            pltpu.VMEM((n_win, BLKS, SUB, LANES), f32),
            pltpu.VMEM((2, SUB, BLKS, SUB, LANES), f32),
            pltpu.VMEM((n_win, BLKS, SUB, LANES), f32),
            pltpu.VMEM((2, 2, BLKS, SUB, LANES), f32),
            pltpu.VMEM((VIEWS, n_win, SUB, LANES), f32),
            pltpu.VMEM((VIEWS, 2, SUB, SUB, LANES), f32),
            pltpu.VMEM((2, BLKS, SUB, LANES), f32),
            pltpu.SMEM(table.shape, jnp.int32),
            pltpu.SemaphoreType.DMA,
        ],
        compiler_params=pltpu.CompilerParams(vmem_limit_bytes=32 << 20),
        name="stereo",
    )(*ins, table)


def xor_front(left_raw, right_raw, line_offset):
    tiles, dets, bands = (lax.axis_size(a) for a in ("tile", "det", "band"))
    lines, width = left_raw.shape

    def fetch(value, flip):
        pairs = []
        for t in range(tiles):
            for d in range(dets):
                for b in range(bands):
                    source = (t * dets + d) * bands + b
                    target = ((t ^ flip) * dets + (d ^ b)) * bands + b
                    pairs.append((source, target))
        return lax.ppermute(value, ("tile", "det", "band"), pairs)

    swap = [(0, 1), (1, 0)]
    both = jnp.concatenate([left_raw, right_raw])
    far, mid, near = (fetch(both, flip) for flip in (3, 2, 1))
    held, line_offset = lax.optimization_barrier((both, line_offset))
    spread = jnp.broadcast_to(line_offset.astype(jnp.float32)[None], (SUB, width))
    slab = jnp.concatenate([held, spread])
    beside = lax.ppermute(slab, "det", swap)
    far2, mid2, near2 = (lax.ppermute(v, "band", swap) for v in (far, mid, near))
    ins = [slab, beside, mid, mid2, near, near2, far, far2]

    def fill(ins, strip, tile, det):
        band = lax.axis_index("band")

        def place(ref, plane, flip, side):
            rows = pl.ds(pl.multiple_of(OMAX + (tile ^ flip) * lines, SUB), lines)
            half = pl.ds(pl.multiple_of((det ^ side) * width, LANES), width)
            strip[plane, rows, half] = ref[plane * lines : (plane + 1) * lines, :]

        slab, beside, mid, mid2, near, near2, far, far2 = ins
        for plane in range(2):
            place(slab, plane, 0, 0)
            place(beside, plane, 0, 1)
            for first, second, flip in ((far, far2, 3), (near, near2, 1), (mid, mid2, 2)):
                if plane or flip != 2:
                    place(first, plane, flip, band)
                    place(second, plane, flip, 1 - band)

    def offsets(ins, det):
        own, other = ins[0], ins[1]
        per = width // LANES
        result = []
        for chunk in range(dets * per):
            cols = slice((chunk % per) * LANES, (chunk % per + 1) * LANES)
            rows = slice(2 * lines, 2 * lines + SUB)
            value = jnp.where(det == chunk // per, own[rows, cols], other[rows, cols])
            result.append(value.astype(jnp.int32))
        return result

    plan = dict(
        lines=lines,
        blocks=tiles,
        two_sided=False,
        pad=0,
        fill=fill,
        offsets=offsets,
        block_of=lambda partner, tile: partner,
    )
    return plan, ins, dets * width


def shift_front(left_raw, right_raw, line_offset):
    count, dets = lax.axis_size("tile"), lax.axis_size("det")
    lines, width = left_raw.shape
    reach = REACH + 1
    own = lax.all_gather(jnp.stack([left_raw, right_raw]), "det")
    offset = lax.all_gather(line_offset, "det").reshape(1, dets * width)
    ins = [offset]
    for shift in range(-reach, reach + 1):
        if shift:
            pairs = [(i, i - shift) for i in range(count) if 0 <= i - shift < count]
            ins.append(lax.ppermute(own, "tile", pairs))
        else:
            ins.append(own)

    def fill(ins, strip, tile, det):
        for j in range(2 * reach + 1):
            rows = slice(OMAX + j * lines, OMAX + (j + 1) * lines)
            for h in range(dets):
                for plane in range(2):
                    strip[plane, rows, h * width : (h + 1) * width] = ins[1 + j][h, plane]

    def offsets(ins, det):
        return [
            jnp.broadcast_to(ins[0][0:1, c * LANES : (c + 1) * LANES], (SUB, LANES))
            for c in range(dets * width // LANES)
        ]

    plan = dict(
        lines=lines,
        blocks=2 * reach + 1,
        two_sided=True,
        pad=SUB,
        fill=fill,
        offsets=offsets,
        block_of=lambda partner, tile: partner - tile + reach,
    )
    return plan, ins, dets * width


def shards(left_raw, right_raw, line_offset, pair_count, pair_tile, pair_base):
    sizes = tuple(lax.axis_size(a) for a in ("tile", "det", "band"))
    front = xor_front if sizes == (4, 2, 2) else shift_front
    plan, ins, cols = front(left_raw, right_raw, line_offset)
    return run_kernel(plan, ins, pair_count, pair_tile, pair_base, cols)


def solution(mesh):
    return jax.shard_map(
        shards,
        mesh=mesh,
        in_specs=(
            P(("groups", "tile"), "det"),
            P(("groups", "tile"), "det"),
            P(("groups", "det")),
            P(("groups", "tile")),
            P(("groups", "tile"), None),
            P(("groups", "tile"), None),
        ),
        out_specs=P(("groups", "tile"), None, "det", None),
        check_vma=False,
    )
```

time: 18.1 us -> 17.8 us (0.983)
  the two profiles are of different devices: /device:TPU:9 before, /device:TPU:0 now
where the time goes in v1:
time: 17.8 us; the launch traced here: 17.7 us
  starting transfers between devices  8.06 us (45%)
  Pallas kernels  5.83 us (33%)
  waiting for transfers between devices  2.31 us (13%)
  local copies, waits for them, and re-layouts  0.76 us (4%)
  between operations  0.7 us (4%)
    pallas_call x1, Pallas kernels, run_kernel(): pl.pallas_call(functools.partial(stereo_kernel, plan), out_shape=jax.Shap...  5.83 us
    ppermute x3, starting transfers between devices, fetch(): return lax.ppermute(value, ('tile', 'det', 'band'), pairs)  5.75 us
    ppermute x1, starting transfers between devices, xor_front(): beside = lax.ppermute(slab, 'det', swap)  1.7 us
    ppermute x3, waiting for transfers between devices, fetch(): return lax.ppermute(value, ('tile', 'det', 'band'), pairs)  1.49 us
    unnamed x9, local copies, waits for them, and re-layouts  0.75 us
    ppermute x3, starting transfers between devices, xor_front(): lax.ppermute(v, 'band', swap)  0.61 us
    ppermute x3, waiting for transfers between devices, xor_front(): lax.ppermute(v, 'band', swap)  0.51 us
  transfers between devices with their start and end apart: 7, of which 4 were waited for; matrix products, arithmetic and copies ran while one was open for 1% of the time, Pallas kernels for 0%

profile of v1, /device:TPU:0, one launch (start us, length us, event | category | flops | bytes accessed | tf_op | source)
XLA Modules:
  0.0 17.7 jit_solution(11976243853256581739)
XLA Ops:
  0.0 0.0 copy-start
  0.0 0.7 %constant_dynamic-update-slice_fusion.1 = f32[32,256]{1,0:T(8,128)S(1)} fusion(f32[16,256]{1,0:T(8,128)} %param.6), kind=kLoop, calls=%fused_computation.2 | loop fusion | bytes 32768
  0.7 0.0 copy-done
  0.7 5.1 %collective-permute-start.5 = (f32[32,256]{1,0:T(8,128)S(1)}, f32[32,256]{1,0:T(8,128)S(1)}, u32[]{:S(2)}, u32[]{:S(2)}) collective-permute-start(f32[32,256]{1,0:T(8,128)S(1)} %constant_dynamic-update-slice_fusion), channel_id=1, source_target_pairs={{0,12},{1,15},{2,14},{3,13},{4,8},{5,11},{6,10},{7,9},{8,4},{9,7},... | collective-permute-start | bytes 98312 | tf_op jit(solution)/shard_map/ppermute | solution.py:349
  5.9 0.0 collective-permute-start.3
  5.9 0.6 %collective-permute-start.1 = (f32[32,256]{1,0:T(8,128)S(1)}, f32[32,256]{1,0:T(8,128)S(1)}, u32[]{:S(2)}, u32[]{:S(2)}) collective-permute-start(f32[32,256]{1,0:T(8,128)S(1)} %constant_dynamic-update-slice_fusion), channel_id=1, source_target_pairs={{0,8},{1,11},{2,10},{3,9},{4,12},{5,15},{6,14},{7,13},{8,0},{9,3},... | collective-permute-start | bytes 98312 | tf_op jit(solution)/shard_map/ppermute | solution.py:349
  6.5 0.0 copy-done.1
  6.5 1.7 %collective-permute-start = (f32[40,256]{1,0:T(8,128)S(1)}, f32[40,256]{1,0:T(8,128)S(1)}, u32[]{:S(2)}, u32[]{:S(2)}) collective-permute-start(f32[40,256]{1,0:T(8,128)S(1)} %pad_maximum_fusion.refs_0_), channel_id=1, source_target_pairs={{0,2},{2,0},{1,3},{3,1},{4,6},{6,4},{5,7},{7,5},{8,10},{10,8},{9,1... | collective-permute-start | bytes 122888 | tf_op jit(solution)/shard_map/ppermute | solution.py:357
  8.9 0.0 copy-start.2
  8.9 0.0 copy-start.3
  8.9 0.0 collective-permute-done.5.refs_6_
  8.9 0.1 collective-permute-start.6
  9.0 0.8 %collective-permute-done.3.refs_4_ = f32[32,256]{1,0:T(8,128)S(1)} collective-permute-done((f32[32,256]{1,0:T(8,128)S(1)}, f32[32,256]{1,0:T(8,128)S(1)}, u32[]{:S(2)}, u32[]{:S(2)}) %collective-permute-start.3) | collective-permute-done | bytes 32800 | tf_op jit(solution)/shard_map/ppermute | solution.py:349
  9.8 0.2 %collective-permute-start.4 = (f32[32,256]{1,0:T(8,128)S(1)}, f32[32,256]{1,0:T(8,128)S(1)}, u32[]{:S(2)}, u32[]{:S(2)}) collective-permute-start(f32[32,256]{1,0:T(8,128)S(1)} %collective-permute-done.3.refs_4_), channel_id=1, source_target_pairs={{0,1},{1,0},{2,3},{3,2},{4,5},{5,4},{6,7},{7,6},{8,9},{9,8},{10,11... | collective-permute-start | bytes 98312 | tf_op jit(solution)/shard_map/ppermute | solution.py:358
  10.0 0.7 %collective-permute-done.1.refs_2_ = f32[32,256]{1,0:T(8,128)S(1)} collective-permute-done((f32[32,256]{1,0:T(8,128)S(1)}, f32[32,256]{1,0:T(8,128)S(1)}, u32[]{:S(2)}, u32[]{:S(2)}) %collective-permute-start.1) | collective-permute-done | bytes 32800 | tf_op jit(solution)/shard_map/ppermute | solution.py:349
  10.7 0.3 %collective-permute-start.2 = (f32[32,256]{1,0:T(8,128)S(1)}, f32[32,256]{1,0:T(8,128)S(1)}, u32[]{:S(2)}, u32[]{:S(2)}) collective-permute-start(f32[32,256]{1,0:T(8,128)S(1)} %collective-permute-done.1.refs_2_), channel_id=1, source_target_pairs={{0,1},{1,0},{2,3},{3,2},{4,5},{5,4},{6,7},{7,6},{8,9},{9,8},{10,11... | collective-permute-start | bytes 98312 | tf_op jit(solution)/shard_map/ppermute | solution.py:358
  11.0 0.0 copy-done.2
  11.0 0.0 copy-done.3
  11.0 0.1 pad_add_fusion.refs_8_
  11.1 0.3 %collective-permute-done.refs_1_ = f32[40,256]{1,0:T(8,128)S(1)} collective-permute-done((f32[40,256]{1,0:T(8,128)S(1)}, f32[40,256]{1,0:T(8,128)S(1)}, u32[]{:S(2)}, u32[]{:S(2)}) %collective-permute-start) | collective-permute-done | bytes 40992 | tf_op jit(solution)/shard_map/ppermute | solution.py:357
  11.4 0.0 collective-permute-done.6.refs_7_
  11.4 0.0 collective-permute-done.4.refs_5_
  11.4 0.5 %collective-permute-done.2.refs_3_ = f32[32,256]{1,0:T(8,128)S(1)} collective-permute-done((f32[32,256]{1,0:T(8,128)S(1)}, f32[32,256]{1,0:T(8,128)S(1)}, u32[]{:S(2)}, u32[]{:S(2)}) %collective-permute-start.2) | collective-permute-done | bytes 32800 | tf_op jit(solution)/shard_map/ppermute | solution.py:358
  11.9 5.8 %stereo.1 = f32[1,2,8,512]{3,2,1,0:T(8,128)} custom-call(f32[40,256]{1,0:T(8,128)S(1)} %pad_maximum_fusion.refs_0_, f32[40,256]{1,0:T(8,128)S(1)} %collective-permute-done.refs_1_, f32[32,256]{1,0:T(8,128)S(1)} %collective-permute-done.1.refs_2_, f32[32,256]{1,0:T(8,128)S(1)} %collective-permute-done.2.refs_3_, ...), custom_call_target="tpu_custom_call" | custom-call | tf_op jit(solution)/shard_map/stereo/pallas_call | solution.py:314
  (5 shorter events, 0.0 us)
Async XLA Ops:
  0.0 0.7 %copy-start = (f32[16,256]{1,0:T(8,128)S(1)}, f32[16,256]{1,0:T(8,128)}, u32[]{:S(2)}) copy-start(f32[16,256]{1,0:T(8,128)} %param.7) | copy-start | bytes 49156
  0.7 5.8 %copy-start.1 = (s32[256]{0:T(256)S(1)}, s32[256]{0:T(256)}, u32[]{:S(2)}) copy-start(s32[256]{0:T(256)} %param.8) | copy-start | bytes 3076
  0.7 8.2 %collective-permute-start.5 = (f32[32,256]{1,0:T(8,128)S(1)}, f32[32,256]{1,0:T(8,128)S(1)}, u32[]{:S(2)}, u32[]{:S(2)}) collective-permute-start(f32[32,256]{1,0:T(8,128)S(1)} %constant_dynamic-update-slice_fusion), channel_id=1, source_target_pairs={{0,12},{1,15},{2,14},{3,13},{4,8},{5,11},{6,10},{7,9},{8,4},{9,7},... | collective-permute-start | bytes 98312 | tf_op jit(solution)/shard_map/ppermute | solution.py:349
  5.9 3.9 %collective-permute-start.3 = (f32[32,256]{1,0:T(8,128)S(1)}, f32[32,256]{1,0:T(8,128)S(1)}, u32[]{:S(2)}, u32[]{:S(2)}) collective-permute-start(f32[32,256]{1,0:T(8,128)S(1)} %constant_dynamic-update-slice_fusion), channel_id=1, source_target_pairs={{0,4},{1,7},{2,6},{3,5},{4,0},{5,3},{6,2},{7,1},{8,12},{9,15},{10,... | collective-permute-start | bytes 98312 | tf_op jit(solution)/shard_map/ppermute | solution.py:349
  5.9 4.8 %collective-permute-start.1 = (f32[32,256]{1,0:T(8,128)S(1)}, f32[32,256]{1,0:T(8,128)S(1)}, u32[]{:S(2)}, u32[]{:S(2)}) collective-permute-start(f32[32,256]{1,0:T(8,128)S(1)} %constant_dynamic-update-slice_fusion), channel_id=1, source_target_pairs={{0,8},{1,11},{2,10},{3,9},{4,12},{5,15},{6,14},{7,13},{8,0},{9,3},... | collective-permute-start | bytes 98312 | tf_op jit(solution)/shard_map/ppermute | solution.py:349
  6.5 4.9 %collective-permute-start = (f32[40,256]{1,0:T(8,128)S(1)}, f32[40,256]{1,0:T(8,128)S(1)}, u32[]{:S(2)}, u32[]{:S(2)}) collective-permute-start(f32[40,256]{1,0:T(8,128)S(1)} %pad_maximum_fusion.refs_0_), channel_id=1, source_target_pairs={{0,2},{2,0},{1,3},{3,1},{4,6},{6,4},{5,7},{7,5},{8,10},{10,8},{9,1... | collective-permute-start | bytes 122888 | tf_op jit(solution)/shard_map/ppermute | solution.py:357
  8.9 2.1 %copy-start.2 = (s32[1,2]{1,0:T(1,128)S(1)}, s32[1,2]{1,0:T(1,128)}, u32[]{:S(2)}) copy-start(s32[1,2]{1,0:T(1,128)} %param.11) | copy-start | bytes 28
  8.9 2.1 %copy-start.3 = (s32[1,2]{1,0:T(1,128)S(1)}, s32[1,2]{1,0:T(1,128)}, u32[]{:S(2)}) copy-start(s32[1,2]{1,0:T(1,128)} %param.10) | copy-start | bytes 28
  8.9 2.5 %collective-permute-start.6 = (f32[32,256]{1,0:T(8,128)S(1)}, f32[32,256]{1,0:T(8,128)S(1)}, u32[]{:S(2)}, u32[]{:S(2)}) collective-permute-start(f32[32,256]{1,0:T(8,128)S(1)} %collective-permute-done.5.refs_6_), channel_id=1, source_target_pairs={{0,1},{1,0},{2,3},{3,2},{4,5},{5,4},{6,7},{7,6},{8,9},{9,8},{10,11... | collective-permute-start | bytes 98312 | tf_op jit(solution)/shard_map/ppermute | solution.py:358
  9.8 1.6 %collective-permute-start.4 = (f32[32,256]{1,0:T(8,128)S(1)}, f32[32,256]{1,0:T(8,128)S(1)}, u32[]{:S(2)}, u32[]{:S(2)}) collective-permute-start(f32[32,256]{1,0:T(8,128)S(1)} %collective-permute-done.3.refs_4_), channel_id=1, source_target_pairs={{0,1},{1,0},{2,3},{3,2},{4,5},{5,4},{6,7},{7,6},{8,9},{9,8},{10,11... | collective-permute-start | bytes 98312 | tf_op jit(solution)/shard_map/ppermute | solution.py:358
  10.7 1.2 %collective-permute-start.2 = (f32[32,256]{1,0:T(8,128)S(1)}, f32[32,256]{1,0:T(8,128)S(1)}, u32[]{:S(2)}, u32[]{:S(2)}) collective-permute-start(f32[32,256]{1,0:T(8,128)S(1)} %collective-permute-done.1.refs_2_), channel_id=1, source_target_pairs={{0,1},{1,0},{2,3},{3,2},{4,5},{5,4},{6,7},{7,6},{8,9},{9,8},{10,11... | collective-permute-start | bytes 98312 | tf_op jit(solution)/shard_map/ppermute | solution.py:358
